TPU v7x, 32 devices: a whole 2x2x4 slice. The times are simulated.
32 devices in a mesh: seq: 2 (over y), ctx: 4 (over z), tp: 4 (over x, core).
Axes of the slice: x: 2, y: 2, z: 4, core: 2. Of those that a mesh axis runs over, the one named last changes fastest.
Arguments:
- tokens: bfloat16 [2048, 2048], P(('seq', 'ctx')), may hold values from -6 to 6
- query_weight: bfloat16 [2048, 2048], P(('seq', 'ctx'), 'tp'), may hold values from -0.125 to 0.125
- key_weight: bfloat16 [2048, 2048], P(('seq', 'ctx'), 'tp'), may hold values from -0.125 to 0.125
- value_weight: bfloat16 [2048, 2048], P(('seq', 'ctx'), 'tp'), may hold values from -0.125 to 0.125
- output_weight: bfloat16 [2048, 2048], P('tp', ('seq', 'ctx')), may hold values from -1.5 to 1.5
- gate_weight: bfloat16 [2048, 8192], P(('seq', 'ctx'), 'tp'), may hold values from -0.125 to 0.125
- up_weight: bfloat16 [2048, 8192], P(('seq', 'ctx'), 'tp'), may hold values from -0.125 to 0.125
- down_weight: bfloat16 [8192, 2048], P('tp', ('seq', 'ctx')), may hold values from -0.0625 to 0.0625
- attention_gain: bfloat16 [2048], P(('seq', 'ctx')), may hold values from 0.25 to 1.75
- feedforward_gain: bfloat16 [2048], P(('seq', 'ctx')), may hold values from 0.25 to 1.75
- order: int32 [8], replicated, may hold values from 0 to 7, each once
- cotangent: bfloat16 [2048, 2048], P(('seq', 'ctx')), may hold values from -6 to 6
Outputs:
- block_output: bfloat16 [2048, 2048], P(('seq', 'ctx'))
- input_grad: float32 [2048, 2048], P(('seq', 'ctx'))
- query_weight_grad: float32 [2048, 2048], P(('seq', 'ctx'), 'tp')
- key_weight_grad: float32 [2048, 2048], P(('seq', 'ctx'), 'tp')
- value_weight_grad: float32 [2048, 2048], P(('seq', 'ctx'), 'tp')
- output_weight_grad: float32 [2048, 2048], P('tp', ('seq', 'ctx'))
- gate_weight_grad: float32 [2048, 8192], P(('seq', 'ctx'), 'tp')
- up_weight_grad: float32 [2048, 8192], P(('seq', 'ctx'), 'tp')
- down_weight_grad: float32 [8192, 2048], P('tp', ('seq', 'ctx'))
- attention_gain_grad: float32 [2048], P(('seq', 'ctx'))
- feedforward_gain_grad: float32 [2048], P(('seq', 'ctx'))
Inputs may be any that keep to these rules, and one draw needn't show every extreme that they name: order holds every block position of a sequence once; the device of ctx index c stores blocks 2c and 2c + 1 of each sequence.
All inputs are finite; a program needn't handle non-finite values.
Results may differ from a plain program's by a relative error of at most 0.02.
Values may be sent and summed in bfloat16 or wider, within the bound.
No kernel may reach another device: no remote copies, remote signals or barrier semaphores. Data moves between devices by JAX's collectives and lax.ppermute only.
A program may use at most 128 MiB of HBM per device.

v0:
```python
from functools import partial
import jax
import jax.numpy as jnp
from jax import lax
from jax.sharding import PartitionSpec as P

HD = 64
BLOCK = 128
THETA = 130000.0
EPS = 1e-05


def shifted(block, axis, distance):
    devices = range(lax.axis_size(axis))
    route = [((i - distance) % len(devices), i) for i in devices]
    return lax.ppermute(block, axis, route)


def rms_norm(hidden, gain):
    return hidden * lax.rsqrt(jnp.mean(hidden * hidden, axis=-1, keepdims=True) + EPS) * gain


def rotary(values, places):
    row_count = values.shape[0]
    by_heads = values.reshape(row_count, -1, HD)
    halfway = HD // 2
    inverse = THETA ** (-(jnp.arange(halfway, dtype=jnp.float32) * 2.0) / HD)
    angle = places.astype(jnp.float32)[:, None] * inverse[None, :]
    angle = jnp.concatenate([angle, angle], axis=1)
    cosine = jnp.cos(angle)[:, None, :]
    sine = jnp.sin(angle)[:, None, :]
    turned = jnp.concatenate([-by_heads[..., halfway:], by_heads[..., :halfway]], axis=-1)
    return (by_heads * cosine + turned * sine).reshape(row_count, -1)


def gated(gate, upward):
    return jax.nn.silu(gate) * upward


def product(left, right):
    return jnp.dot(left, right, preferred_element_type=jnp.float32)


def contract_rows(left, right):
    return lax.dot_general(
        left, right, (((0,), (0,)), ((), ())), preferred_element_type=jnp.float32
    )


def contract_cols(left, right):
    return lax.dot_general(
        left, right, (((1,), (1,)), ((), ())), preferred_element_type=jnp.float32
    )


def key_places(order, first_row, row_total):
    stored = first_row + jnp.arange(row_total, dtype=jnp.int32)
    group_slot = stored // BLOCK
    slot_table = jnp.arange(order.shape[0], dtype=jnp.int32)
    block_place = jnp.sum(
        jnp.where(group_slot[:, None] == slot_table[None, :], order[None, :], 0), axis=1
    )
    return block_place * BLOCK + stored % BLOCK


def exp_scores(query_heads, query_places, key_rows, key_pos):
    row_total = key_rows.shape[0]
    key_heads = key_rows.reshape(row_total, -1, HD)
    scores = (
        jnp.einsum("qhd,khd->hqk", query_heads, key_heads, preferred_element_type=jnp.float32)
        * 0.125
    )
    allowed = query_places[:, None] >= key_pos[None, :]
    return (jnp.where(allowed[None], jnp.exp(scores), 0.0), key_heads)


def per_device(
    tokens,
    query_weight,
    key_weight,
    value_weight,
    output_weight,
    gate_weight,
    up_weight,
    down_weight,
    attention_gain,
    feedforward_gain,
    order,
    cotangent,
):
    rows_local = tokens.shape[0]
    ctx_index = lax.axis_index("ctx")
    ctx_total = lax.axis_size("ctx")
    gathered = (
        lax.all_gather(query_weight, ("seq", "ctx"), axis=0, tiled=True),
        lax.all_gather(key_weight, ("seq", "ctx"), axis=0, tiled=True),
        lax.all_gather(value_weight, ("seq", "ctx"), axis=0, tiled=True),
        lax.all_gather(output_weight, ("seq", "ctx"), axis=1, tiled=True),
        lax.all_gather(gate_weight, ("seq", "ctx"), axis=0, tiled=True),
        lax.all_gather(up_weight, ("seq", "ctx"), axis=0, tiled=True),
        lax.all_gather(down_weight, ("seq", "ctx"), axis=1, tiled=True),
        lax.all_gather(attention_gain, ("seq", "ctx"), axis=0, tiled=True),
        lax.all_gather(feedforward_gain, ("seq", "ctx"), axis=0, tiled=True),
    )
    (
        full_query,
        full_key,
        full_value,
        full_output,
        full_gate,
        full_up,
        full_down,
        gain_first,
        gain_second,
    ) = gathered
    inputs = tokens.astype(jnp.float32)
    query_places = key_places(order, ctx_index * rows_local, rows_local)
    normed_value, norm_back_first = jax.vjp(rms_norm, inputs, gain_first.astype(jnp.float32))
    normed = normed_value.astype(jnp.bfloat16)
    rope_here = partial(rotary, places=query_places)
    query_rot, query_back = jax.vjp(rope_here, product(normed, full_query))
    key_rot, key_back = jax.vjp(rope_here, product(normed, full_key))
    value_rows = product(normed, full_value).astype(jnp.bfloat16)
    query_rows = query_rot.astype(jnp.bfloat16)
    key_rows = key_rot.astype(jnp.bfloat16)
    width = query_rows.shape[1]
    head_count = width // HD
    query_heads = query_rows.reshape(rows_local, head_count, HD)
    packed = jnp.stack([key_rows, value_rows])
    empty_totals = jnp.zeros((rows_local, head_count), jnp.float32)
    empty_numerator = jnp.zeros((rows_local, width), jnp.float32)
    arrived = lax.all_gather(packed, "ctx", axis=1, tiled=True)
    row_total = arrived.shape[1]

    def one_block(block_index, partial_state):
        first_row = block_index * rows_local
        section = lax.dynamic_slice_in_dim(arrived, first_row, rows_local, 1)
        key_pos = key_places(order, first_row, rows_local)
        weights, key_heads = exp_scores(query_heads, query_places, section[0], key_pos)
        value_heads = section[1].reshape(rows_local, -1, HD)
        totals, numerator = partial_state
        totals = totals + jnp.sum(weights, axis=2).T
        numerator = numerator + jnp.einsum(
            "hqk,khd->qhd",
            weights.astype(jnp.bfloat16),
            value_heads,
            preferred_element_type=jnp.float32,
        ).reshape(rows_local, width)
        return (totals, numerator)

    totals, numerator = lax.fori_loop(
        0, row_total // rows_local, one_block, (empty_totals, empty_numerator)
    )
    numerator_heads = numerator.reshape(rows_local, head_count, HD)
    mixed = (numerator_heads / totals[:, :, None]).astype(jnp.bfloat16).reshape(rows_local, width)
    middle = inputs + lax.psum(product(mixed, full_output), "tp")
    normed_two_value, norm_back_second = jax.vjp(rms_norm, middle, gain_second.astype(jnp.float32))
    normed_two = normed_two_value.astype(jnp.bfloat16)
    activated, gated_back = jax.vjp(
        gated, product(normed_two, full_gate), product(normed_two, full_up)
    )
    hidden = activated.astype(jnp.bfloat16)
    block_output = middle + lax.psum(product(hidden, full_down).astype(jnp.bfloat16), "tp").astype(
        jnp.float32
    )
    back_weights = (
        lax.all_gather(query_weight, ("seq", "ctx"), axis=0, tiled=True),
        lax.all_gather(key_weight, ("seq", "ctx"), axis=0, tiled=True),
        lax.all_gather(value_weight, ("seq", "ctx"), axis=0, tiled=True),
        lax.all_gather(output_weight, ("seq", "ctx"), axis=1, tiled=True),
        lax.all_gather(gate_weight, ("seq", "ctx"), axis=0, tiled=True),
        lax.all_gather(up_weight, ("seq", "ctx"), axis=0, tiled=True),
        lax.all_gather(down_weight, ("seq", "ctx"), axis=1, tiled=True),
        lax.all_gather(attention_gain, ("seq", "ctx"), axis=0, tiled=True),
        lax.all_gather(feedforward_gain, ("seq", "ctx"), axis=0, tiled=True),
    )
    (
        back_query,
        back_key,
        back_value,
        back_output,
        back_gate,
        back_up,
        back_down,
        gain_unused,
        gain_spare,
    ) = back_weights
    down_grad = contract_rows(hidden, cotangent)
    hidden_grad = contract_cols(cotangent, back_down)
    gate_grad, upward_grad = gated_back(hidden_grad)
    gate_grad = gate_grad.astype(jnp.bfloat16)
    upward_grad = upward_grad.astype(jnp.bfloat16)
    gate_wgrad = contract_rows(normed_two, gate_grad)
    upward_wgrad = contract_rows(normed_two, upward_grad)
    normed_two_grad = lax.psum(
        contract_cols(gate_grad, back_gate) + contract_cols(upward_grad, back_up), "tp"
    )
    middle_norm_grad, second_gain_grad = norm_back_second(normed_two_grad)
    middle_grad = cotangent.astype(jnp.float32) + middle_norm_grad
    branch_grad = middle_grad.astype(jnp.bfloat16)
    output_wgrad = contract_rows(mixed, branch_grad)
    mixed_grad = contract_cols(branch_grad, back_output).reshape(rows_local, head_count, HD)
    numerator_grad = (mixed_grad / totals[:, :, None]).astype(jnp.bfloat16)
    totals_grad = -jnp.sum(mixed_grad * numerator_heads, axis=2) / (totals * totals)
    totals_grad_heads = totals_grad.T[:, :, None]

    def visit(turn_index, state):
        visiting, carried, query_acc = state
        source = (ctx_index - turn_index) % ctx_total
        key_pos = key_places(order, source * rows_local, rows_local)
        weights, key_heads = exp_scores(query_heads, query_places, visiting[0], key_pos)
        value_heads = visiting[1].reshape(rows_local, -1, HD)
        through = jnp.einsum(
            "qhd,khd->hqk", numerator_grad, value_heads, preferred_element_type=jnp.float32
        )
        slopes = (weights * (through + totals_grad_heads)).astype(jnp.bfloat16)
        query_acc = (
            query_acc
            + jnp.einsum("hqk,khd->qhd", slopes, key_heads, preferred_element_type=jnp.float32)
            * 0.125
        )
        key_term = (
            jnp.einsum("hqk,qhd->khd", slopes, query_heads, preferred_element_type=jnp.float32)
            * 0.125
        )
        value_term = jnp.einsum(
            "hqk,qhd->khd",
            weights.astype(jnp.bfloat16),
            numerator_grad,
            preferred_element_type=jnp.float32,
        )
        carried = carried + jnp.stack(
            [key_term.reshape(rows_local, width), value_term.reshape(rows_local, width)]
        )
        visiting = shifted(visiting, "ctx", 1)
        carried = shifted(carried, "ctx", 1)
        return (visiting, carried, query_acc)

    start_state = (
        packed,
        jnp.zeros((2, rows_local, width), jnp.float32),
        jnp.zeros((rows_local, head_count, HD), jnp.float32),
    )
    ended, key_value_grad, query_acc = lax.fori_loop(0, ctx_total, visit, start_state)
    query_proj_grad = query_back(query_acc.reshape(rows_local, width))[0].astype(jnp.bfloat16)
    key_proj_grad = key_back(key_value_grad[0])[0].astype(jnp.bfloat16)
    value_grad = key_value_grad[1].astype(jnp.bfloat16)
    query_wgrad = contract_rows(normed, query_proj_grad)
    key_wgrad = contract_rows(normed, key_proj_grad)
    value_wgrad = contract_rows(normed, value_grad)
    normed_grad = lax.psum(
        (
            contract_cols(query_proj_grad, back_query)
            + contract_cols(key_proj_grad, back_key)
            + contract_cols(value_grad, back_value)
        ).astype(jnp.bfloat16),
        "tp",
    ).astype(jnp.float32)
    input_norm_grad, first_gain_grad = norm_back_first(normed_grad)
    input_grad = middle_grad + input_norm_grad
    scattered = (
        lax.psum_scatter(
            query_wgrad.astype(jnp.bfloat16), ("seq", "ctx"), scatter_dimension=0, tiled=True
        ).astype(jnp.float32),
        lax.psum_scatter(
            key_wgrad.astype(jnp.bfloat16), ("seq", "ctx"), scatter_dimension=0, tiled=True
        ).astype(jnp.float32),
        lax.psum_scatter(
            value_wgrad.astype(jnp.bfloat16), ("seq", "ctx"), scatter_dimension=0, tiled=True
        ).astype(jnp.float32),
        lax.psum_scatter(
            output_wgrad.astype(jnp.bfloat16), ("seq", "ctx"), scatter_dimension=1, tiled=True
        ).astype(jnp.float32),
        lax.psum_scatter(
            gate_wgrad.astype(jnp.bfloat16), ("seq", "ctx"), scatter_dimension=0, tiled=True
        ).astype(jnp.float32),
        lax.psum_scatter(
            upward_wgrad.astype(jnp.bfloat16), ("seq", "ctx"), scatter_dimension=0, tiled=True
        ).astype(jnp.float32),
        lax.psum_scatter(
            down_grad.astype(jnp.bfloat16), ("seq", "ctx"), scatter_dimension=1, tiled=True
        ).astype(jnp.float32),
        lax.psum_scatter(
            first_gain_grad.astype(jnp.bfloat16), ("seq", "ctx"), scatter_dimension=0, tiled=True
        ).astype(jnp.float32),
        lax.psum_scatter(
            second_gain_grad.astype(jnp.bfloat16), ("seq", "ctx"), scatter_dimension=0, tiled=True
        ).astype(jnp.float32),
    )
    return (
        block_output.astype(jnp.bfloat16),
        input_grad,
        scattered[0],
        scattered[1],
        scattered[2],
        scattered[3],
        scattered[4],
        scattered[5],
        scattered[6],
        scattered[7],
        scattered[8],
    )


def solution(mesh):
    placed = (
        P(("seq", "ctx"), None),
        P(("seq", "ctx"), "tp"),
        P(("seq", "ctx"), "tp"),
        P(("seq", "ctx"), "tp"),
        P("tp", ("seq", "ctx")),
        P(("seq", "ctx"), "tp"),
        P(("seq", "ctx"), "tp"),
        P("tp", ("seq", "ctx")),
        P(("seq", "ctx")),
        P(("seq", "ctx")),
        P(),
        P(("seq", "ctx"), None),
    )
    return jax.shard_map(
        per_device,
        mesh=mesh,
        in_specs=placed,
        out_specs=(
            P(("seq", "ctx"), None),
            P(("seq", "ctx"), None),
            P(("seq", "ctx"), "tp"),
            P(("seq", "ctx"), "tp"),
            P(("seq", "ctx"), "tp"),
            P("tp", ("seq", "ctx")),
            P(("seq", "ctx"), "tp"),
            P(("seq", "ctx"), "tp"),
            P("tp", ("seq", "ctx")),
            P(("seq", "ctx")),
            P(("seq", "ctx")),
        ),
        check_vma=False,
    )
```

profile of v0, /device:TPU:0, one launch (start us, length us, event | category | flops | bytes accessed | tf_op | source)
XLA Modules:
  0.0 1750.2 jit_solution(15163281541108414726)
XLA Ops:
  10.1 22.3 %all-gather = bf16[8,1,256]{2,1,0:T(2,128)(2,1)S(1)} all-gather(bf16[1,1,256]{2,1,0:T(2,128)(2,1)S(1)} %reshape.359), channel_id=1, replica_groups=mesh['seq'=2,'ctx'=4,'tp'=4] {'seq','ctx'}, dimensions={0}, use_global_device_ids=true | all-gather | bytes 4608 | tf_op jit(solution)/shard_map/all_gather | solution.py:102
  34.6 27.6 %all-gather.11.cloned.1.call-done = bf16[2048,512]{1,0:T(8,128)(2,1)} async-done(((bf16[256,512]{1,0:T(8,128)(2,1)}), bf16[2048,512]{1,0:T(8,128)(2,1)}) %all-gather.11.cloned.1.call-update) | async-done | bytes 2097168 | tf_op jit(solution)/shard_map/all_gather | solution.py:96
  64.7 47.4 %all-gather.17.cloned.1.call-done = bf16[2048,512]{1,0:T(8,128)(2,1)} async-done(((bf16[256,512]{1,0:T(8,128)(2,1)}), bf16[2048,512]{1,0:T(8,128)(2,1)}) %all-gather.17.cloned.1.call-update) | async-done | bytes 2097168 | tf_op jit(solution)/shard_map/all_gather | solution.py:95
  123.1 39.0 %all-gather.13.cloned.1.call-done = bf16[2048,512]{1,0:T(8,128)(2,1)} async-done(((bf16[256,512]{1,0:T(8,128)(2,1)}), bf16[2048,512]{1,0:T(8,128)(2,1)}) %all-gather.13.cloned.1.call-update) | async-done | bytes 2097168 | tf_op jit(solution)/shard_map/all_gather | solution.py:97
  166.1 43.8 %all-gather.15.cloned.1.call-done = bf16[2,1024,512]{2,1,0:T(8,128)(2,1)} async-done(((bf16[2,256,512]{2,1,0:T(8,128)(2,1)}), bf16[2,1024,512]{2,1,0:T(8,128)(2,1)}) %all-gather.15.cloned.1.call-update) | async-done | bytes 2097168 | tf_op jit(solution)/shard_map/all_gather | solution.py:132
  209.9 22.9 %while.39 = (s32[]{:T(128)}, f32[256,8]{0,1:T(8,128)S(1)}, f32[256,512]{0,1:T(8,128)}, s32[256]{0:T(256)}, s32[8]{0:T(128)}, /*index=5*/bf16[2,1024,512]{2,1,0:T...) while((s32[]{:T(128)}, f32[256,8]{0,1:T(8,128)S(1)}, ...), condition=%wide.region_5.6_spmd.clone, body=%wide.region_2.5_spmd.clone.sunk | while | flops 137706752 | bytes 9411818 | solution.py:151
  233.8 27.7 %all-gather.19.cloned.1.call-done = bf16[512,2048]{1,0:T(8,128)(2,1)} async-done(((bf16[512,256]{1,0:T(8,128)(2,1)}), bf16[512,2048]{1,0:T(8,128)(2,1)}) %all-gather.19.cloned.1.call-update) | async-done | bytes 2097168 | tf_op jit(solution)/shard_map/all_gather | solution.py:98
  267.5 18.2 %all-gather.1 = bf16[8,1,256]{2,1,0:T(2,128)(2,1)S(1)} all-gather(bf16[1,1,256]{2,1,0:T(2,128)(2,1)S(1)} %reshape.361), channel_id=1, replica_groups=mesh['seq'=2,'ctx'=4,'tp'=4] {'seq','ctx'}, dimensions={0}, use_global_device_ids=true | all-gather | bytes 4608 | tf_op jit(solution)/shard_map/all_gather | solution.py:103
  286.3 28.6 %all-reduce.12.cloned.1.call-done = f32[256,2048]{1,0:T(8,128)} async-done(((f32[256,2048]{1,0:T(8,128)}), f32[256,2048]{1,0:T(8,128)}) %all-reduce.12.cloned.1.call-update) | async-done | bytes 2097168 | tf_op jit(solution)/shard_map/psum | solution.py:156
  317.8 124.5 %all-gather.21.cloned.1.call-done = bf16[2048,2048]{1,0:T(8,128)(2,1)} async-done(((bf16[256,2048]{1,0:T(8,128)(2,1)}), bf16[2048,2048]{1,0:T(8,128)(2,1)}) %all-gather.21.cloned.1.call-update) | async-done | bytes 8388624 | tf_op jit(solution)/shard_map/all_gather | solution.py:99
  442.3 7.0 fusion.66
  449.3 118.5 %all-gather.23.cloned.1.call-done = bf16[2048,2048]{1,0:T(8,128)(2,1)} async-done(((bf16[256,2048]{1,0:T(8,128)(2,1)}), bf16[2048,2048]{1,0:T(8,128)(2,1)}) %all-gather.23.cloned.1.call-update) | async-done | bytes 8388624 | tf_op jit(solution)/shard_map/all_gather | solution.py:100
  567.8 7.0 fusion.67
  574.8 118.8 %all-gather.25.cloned.1.call-done = bf16[2048,2048]{1,0:T(8,128)(2,1)} async-done(((bf16[2048,256]{1,0:T(8,128)(2,1)}), bf16[2048,2048]{1,0:T(8,128)(2,1)}) %all-gather.25.cloned.1.call-update) | async-done | bytes 8388624 | tf_op jit(solution)/shard_map/all_gather | solution.py:101
  693.6 9.0 multiply_convert_fusion.1
  702.6 6.6 fusion.68
  714.9 7.4 convolution_convert_fusion.7
  722.4 40.2 %all-reduce.14.cloned.1.call-done = f32[256,2048]{1,0:T(8,128)} async-done(((f32[256,2048]{1,0:T(8,128)}), f32[256,2048]{1,0:T(8,128)}) %all-reduce.14.cloned.1.call-update) | async-done | bytes 2097168 | tf_op jit(solution)/shard_map/psum | solution.py:195
  768.8 173.2 %while.40 = (s32[]{:T(128)}, bf16[2,256,512]{1,2,0:T(8,128)(2,1)}, f32[2,256,512]{1,2,0:T(8,128)S(1)}, f32[256,8,64]{0,2,1:T(8,128)}, s32[256]{0:T(256)}, /*inde...) while((s32[]{:T(128)}, bf16[2,256,512]{1,2,0:T(8,128)(2,1)}, ...), condition=%wide.region_14.15_spmd.clone, body=%wide.region_12.14_spmd.clone.sunk | while | flops 340866304 | bytes 25116048 | solution.py:244
  779.5 34.0 %collective-permute-done = bf16[2,256,512]{1,2,0:T(8,128)(2,1)} collective-permute-done((bf16[2,256,512]{1,2,0:T(8,128)(2,1)S(1)}, bf16[2,256,512]{1,2,0:T(8,128)(2,1)}, u32[]{:S(2)}, u32[]{:S(2)}) %collective-permute-start) | collective-permute-done | bytes 524320 | tf_op jit(solution)/shard_map/while/body/eval_jaxpr/ppermute | solution.py:16
  823.4 33.8 %collective-permute-done = bf16[2,256,512]{1,2,0:T(8,128)(2,1)} collective-permute-done((bf16[2,256,512]{1,2,0:T(8,128)(2,1)S(1)}, bf16[2,256,512]{1,2,0:T(8,128)(2,1)}, u32[]{:S(2)}, u32[]{:S(2)}) %collective-permute-start) | collective-permute-done | bytes 524320 | tf_op jit(solution)/shard_map/while/body/eval_jaxpr/ppermute | solution.py:16
  866.0 34.1 %collective-permute-done = bf16[2,256,512]{1,2,0:T(8,128)(2,1)} collective-permute-done((bf16[2,256,512]{1,2,0:T(8,128)(2,1)S(1)}, bf16[2,256,512]{1,2,0:T(8,128)(2,1)}, u32[]{:S(2)}, u32[]{:S(2)}) %collective-permute-start) | collective-permute-done | bytes 524320 | tf_op jit(solution)/shard_map/while/body/eval_jaxpr/ppermute | solution.py:16
  908.9 33.2 %collective-permute-done = bf16[2,256,512]{1,2,0:T(8,128)(2,1)} collective-permute-done((bf16[2,256,512]{1,2,0:T(8,128)(2,1)S(1)}, bf16[2,256,512]{1,2,0:T(8,128)(2,1)}, u32[]{:S(2)}, u32[]{:S(2)}) %collective-permute-start) | collective-permute-done | bytes 524320 | tf_op jit(solution)/shard_map/while/body/eval_jaxpr/ppermute | solution.py:16
  985.6 13.9 all-reduce.16.cloned.1.call-done
  1001.8 22.1 %all-reduce.6 = (bf16[2048]{0:T(1024)(128)(2,1)S(1)}, bf16[2048]{0:T(1024)(128)(2,1)S(1)}) all-reduce(bf16[2048]{0:T(1024)(128)(2,1)S(1)} %get-tuple-element.603, bf16[2048]{0:T(1024)(128)(2,1)S(1)} %copy-done.34), channel_id=9, replica_groups=mesh['seq'=2,'ctx'=4,'tp'=4] {'seq','ctx'}, use_global_device_ids=true, to_apply=%region_25.26.clone | all-reduce | flops 4096 | bytes 16384
  1029.8 42.1 %reduce-scatter.14.cloned.1.call-done = bf16[512,256]{1,0:T(8,128)(2,1)} async-done(((bf16[512,2048]{1,0:T(8,128)(2,1)}), bf16[512,256]{1,0:T(8,128)(2,1)}) %reduce-scatter.14.cloned.1.call-update) | async-done | bytes 262160 | tf_op jit(solution)/shard_map/reduce_scatter | solution.py:271
  1073.7 69.6 %reduce-scatter.8.cloned.1.call-done = bf16[256,512]{1,0:T(8,128)(2,1)} async-done(((bf16[2048,512]{1,0:T(8,128)(2,1)}), bf16[256,512]{1,0:T(8,128)(2,1)}) %reduce-scatter.8.cloned.1.call-update) | async-done | bytes 262160 | tf_op jit(solution)/shard_map/reduce_scatter | solution.py:262
  1145.1 68.9 %reduce-scatter.10.cloned.1.call-done = bf16[256,512]{1,0:T(8,128)(2,1)} async-done(((bf16[2048,512]{1,0:T(8,128)(2,1)}), bf16[256,512]{1,0:T(8,128)(2,1)}) %reduce-scatter.10.cloned.1.call-update) | async-done | bytes 262160 | tf_op jit(solution)/shard_map/reduce_scatter | solution.py:265
  1215.7 68.9 %reduce-scatter.12.cloned.1.call-done = bf16[256,512]{1,0:T(8,128)(2,1)} async-done(((bf16[2048,512]{1,0:T(8,128)(2,1)}), bf16[256,512]{1,0:T(8,128)(2,1)}) %reduce-scatter.12.cloned.1.call-update) | async-done | bytes 262160 | tf_op jit(solution)/shard_map/reduce_scatter | solution.py:268
  1286.4 150.1 %reduce-scatter.16.cloned.1.call-done = bf16[256,2048]{1,0:T(8,128)(2,1)} async-done(((bf16[2048,2048]{1,0:T(8,128)(2,1)}), bf16[256,2048]{1,0:T(8,128)(2,1)}) %reduce-scatter.16.cloned.1.call-update) | async-done | bytes 1048592 | tf_op jit(solution)/shard_map/reduce_scatter | solution.py:274
  1439.3 148.7 %reduce-scatter.18.cloned.1.call-done = bf16[256,2048]{1,0:T(8,128)(2,1)} async-done(((bf16[2048,2048]{1,0:T(8,128)(2,1)}), bf16[256,2048]{1,0:T(8,128)(2,1)}) %reduce-scatter.18.cloned.1.call-update) | async-done | bytes 1048592 | tf_op jit(solution)/shard_map/reduce_scatter | solution.py:277
  1590.8 149.6 %reduce-scatter.20.cloned.1.call-done = bf16[2048,256]{1,0:T(8,128)(2,1)} async-done(((bf16[2048,2048]{1,0:T(8,128)(2,1)}), bf16[2048,256]{1,0:T(8,128)(2,1)}) %reduce-scatter.20.cloned.1.call-update) | async-done | bytes 1048592 | tf_op jit(solution)/shard_map/reduce_scatter | solution.py:280
  (296 shorter events, 171.6 us)
Async XLA Ops:
  7.2 55.0 %all-gather.11.cloned.1.call-start = ((), (), s32[]{:S(2)}) async-start(), calls=%async_computation.7 | async-start | bytes 2359296 | tf_op jit(solution)/shard_map/all_gather | solution.py:96
  7.9 104.2 %all-gather.17.cloned.1.call-start = ((), (), s32[]{:S(2)}) async-start(), calls=%async_computation.10 | async-start | bytes 2359296 | tf_op jit(solution)/shard_map/all_gather | solution.py:95
  8.7 153.4 %all-gather.13.cloned.1.call-start = ((), (), s32[]{:S(2)}) async-start(), calls=%async_computation.8 | async-start | bytes 2359296 | tf_op jit(solution)/shard_map/all_gather | solution.py:97
  9.4 200.5 %all-gather.15.cloned.1.call-start = ((), (), s32[]{:S(2)}) async-start(), calls=%async_computation.9 | async-start | bytes 2621440 | tf_op jit(solution)/shard_map/all_gather | solution.py:132
  34.6 127.5 %copy-start.30 = (f32[256]{0:T(256)}, f32[256]{0:T(256)S(1)}, u32[]{:S(2)}) copy-start(f32[256]{0:T(256)S(1)} %fusion.49) | copy-start | bytes 3076
  165.3 96.2 %all-gather.19.cloned.1.call-start = ((), (), s32[]{:S(2)}) async-start(), calls=%async_computation.11 | async-start | bytes 2359296 | tf_op jit(solution)/shard_map/all_gather | solution.py:98
  165.9 149.0 %all-reduce.12.cloned.1.call-start = ((), (), s32[]{:S(2)}) async-start(), calls=%async_computation.12 | async-start | bytes 4194304 | tf_op jit(solution)/shard_map/psum | solution.py:156
  265.2 49.7 %copy-start.3 = (bf16[256,2048]{1,0:T(8,128)(2,1)S(1)}, bf16[256,2048]{1,0:T(8,128)(2,1)}, u32[]{:S(2)}) copy-start(bf16[256,2048]{1,0:T(8,128)(2,1)} %param.16) | copy-start | bytes 3145732
  265.2 177.1 %all-gather.21.cloned.1.call-start = ((), (), s32[]{:S(2)}) async-start(), calls=%async_computation.13 | async-start | bytes 9437184 | tf_op jit(solution)/shard_map/all_gather | solution.py:99
  266.0 301.8 %all-gather.23.cloned.1.call-start = ((), (), s32[]{:S(2)}) async-start(), calls=%async_computation.14 | async-start | bytes 9437184 | tf_op jit(solution)/shard_map/all_gather | solution.py:100
  266.7 426.9 %all-gather.25.cloned.1.call-start = ((), (), s32[]{:S(2)}) async-start(), calls=%async_computation.15 | async-start | bytes 9437184 | tf_op jit(solution)/shard_map/all_gather | solution.py:101
  267.5 495.2 %all-reduce.14.cloned.1.call-start = ((), (), s32[]{:S(2)}) async-start(), calls=%async_computation.16 | async-start | bytes 4194304 | tf_op jit(solution)/shard_map/psum | solution.py:195
  316.9 448.6 %copy-start = (f32[256,2048]{1,0:T(8,128)}, f32[256,2048]{1,0:T(8,128)S(1)}, u32[]{:S(2)}) copy-start(f32[256,2048]{1,0:T(8,128)S(1)} %get-tuple-element.644) | copy-start | bytes 6291460
  317.8 250.0 %copy-start.9 = (bf16[256,2048]{1,0:T(8,128)(2,1)}, bf16[256,2048]{1,0:T(8,128)(2,1)S(1)}, u32[]{:S(2)}) copy-start(bf16[256,2048]{1,0:T(8,128)(2,1)S(1)} %multiply_convert_fusion.3) | copy-start | bytes 3145732
  712.9 286.6 %all-reduce.16.cloned.1.call-start = ((), (), s32[]{:S(2)}) async-start(), calls=%async_computation.24 | async-start | bytes 4194304 | tf_op jit(solution)/shard_map/psum | solution.py:163
  714.9 47.7 %copy-start.29 = (f32[8,1,256]{2,1,0:T(1,128)S(1)}, f32[8,1,256]{2,1,0:T(1,128)}, u32[]{:S(2)}) copy-start(f32[8,1,256]{2,1,0:T(1,128)} %convert_element_type.216) | copy-start | bytes 24580
  714.9 47.7 %copy-start.33 = (f32[256]{0:T(256)S(1)}, f32[256]{0:T(256)}, u32[]{:S(2)}) copy-start(f32[256]{0:T(256)} %copy-done.32) | copy-start | bytes 3076
  775.3 38.2 %collective-permute-start.1 = (f32[2,256,512]{1,2,0:T(8,128)}, f32[2,256,512]{1,2,0:T(8,128)S(1)}, u32[]{:S(2)}, u32[]{:S(2)}) collective-permute-start(f32[2,256,512]{1,2,0:T(8,128)} %maximum_add_fusion.2), channel_id=1, source_target_pairs={{12,0},{0,4},{4,8},{8,12},{13,1},{1,5},{5,9},{9,13},{14,2},{2,6},{... | collective-permute-start | bytes 3145736 | tf_op jit(solution)/shard_map/while/body/eval_jaxpr/ppermute | solution.py:16
  776.8 36.7 %collective-permute-start = (bf16[2,256,512]{1,2,0:T(8,128)(2,1)S(1)}, bf16[2,256,512]{1,2,0:T(8,128)(2,1)}, u32[]{:S(2)}, u32[]{:S(2)}) collective-permute-start(bf16[2,256,512]{1,2,0:T(8,128)(2,1)S(1)} %copy.95), channel_id=1, source_target_pairs={{12,0},{0,4},{4,8},{8,12},{13,1},{1,5},{5,9},{9,13},{14,2},{2,6},{... | collective-permute-start | bytes 1572872 | tf_op jit(solution)/shard_map/while/body/eval_jaxpr/ppermute | solution.py:16
  820.0 37.3 %collective-permute-start.1 = (f32[2,256,512]{1,2,0:T(8,128)}, f32[2,256,512]{1,2,0:T(8,128)S(1)}, u32[]{:S(2)}, u32[]{:S(2)}) collective-permute-start(f32[2,256,512]{1,2,0:T(8,128)} %maximum_add_fusion.2), channel_id=1, source_target_pairs={{12,0},{0,4},{4,8},{8,12},{13,1},{1,5},{5,9},{9,13},{14,2},{2,6},{... | collective-permute-start | bytes 3145736 | tf_op jit(solution)/shard_map/while/body/eval_jaxpr/ppermute | solution.py:16
  820.0 37.3 %collective-permute-start = (bf16[2,256,512]{1,2,0:T(8,128)(2,1)S(1)}, bf16[2,256,512]{1,2,0:T(8,128)(2,1)}, u32[]{:S(2)}, u32[]{:S(2)}) collective-permute-start(bf16[2,256,512]{1,2,0:T(8,128)(2,1)S(1)} %copy.95), channel_id=1, source_target_pairs={{12,0},{0,4},{4,8},{8,12},{13,1},{1,5},{5,9},{9,13},{14,2},{2,6},{... | collective-permute-start | bytes 1572872 | tf_op jit(solution)/shard_map/while/body/eval_jaxpr/ppermute | solution.py:16
  863.8 36.4 %collective-permute-start.1 = (f32[2,256,512]{1,2,0:T(8,128)}, f32[2,256,512]{1,2,0:T(8,128)S(1)}, u32[]{:S(2)}, u32[]{:S(2)}) collective-permute-start(f32[2,256,512]{1,2,0:T(8,128)} %maximum_add_fusion.2), channel_id=1, source_target_pairs={{12,0},{0,4},{4,8},{8,12},{13,1},{1,5},{5,9},{9,13},{14,2},{2,6},{... | collective-permute-start | bytes 3145736 | tf_op jit(solution)/shard_map/while/body/eval_jaxpr/ppermute | solution.py:16
  863.8 36.4 %collective-permute-start = (bf16[2,256,512]{1,2,0:T(8,128)(2,1)S(1)}, bf16[2,256,512]{1,2,0:T(8,128)(2,1)}, u32[]{:S(2)}, u32[]{:S(2)}) collective-permute-start(bf16[2,256,512]{1,2,0:T(8,128)(2,1)S(1)} %copy.95), channel_id=1, source_target_pairs={{12,0},{0,4},{4,8},{8,12},{13,1},{1,5},{5,9},{9,13},{14,2},{2,6},{... | collective-permute-start | bytes 1572872 | tf_op jit(solution)/shard_map/while/body/eval_jaxpr/ppermute | solution.py:16
  906.6 35.5 %collective-permute-start.1 = (f32[2,256,512]{1,2,0:T(8,128)}, f32[2,256,512]{1,2,0:T(8,128)S(1)}, u32[]{:S(2)}, u32[]{:S(2)}) collective-permute-start(f32[2,256,512]{1,2,0:T(8,128)} %maximum_add_fusion.2), channel_id=1, source_target_pairs={{12,0},{0,4},{4,8},{8,12},{13,1},{1,5},{5,9},{9,13},{14,2},{2,6},{... | collective-permute-start | bytes 3145736 | tf_op jit(solution)/shard_map/while/body/eval_jaxpr/ppermute | solution.py:16
  906.6 35.5 %collective-permute-start = (bf16[2,256,512]{1,2,0:T(8,128)(2,1)S(1)}, bf16[2,256,512]{1,2,0:T(8,128)(2,1)}, u32[]{:S(2)}, u32[]{:S(2)}) collective-permute-start(bf16[2,256,512]{1,2,0:T(8,128)(2,1)S(1)} %copy.95), channel_id=1, source_target_pairs={{12,0},{0,4},{4,8},{8,12},{13,1},{1,5},{5,9},{9,13},{14,2},{2,6},{... | collective-permute-start | bytes 1572872 | tf_op jit(solution)/shard_map/while/body/eval_jaxpr/ppermute | solution.py:16
  949.9 122.0 %reduce-scatter.14.cloned.1.call-start = ((), (), s32[]{:S(2)}) async-start(), calls=%async_computation.20 | async-start | bytes 2359296 | tf_op jit(solution)/shard_map/reduce_scatter | solution.py:271
  954.5 188.8 %reduce-scatter.8.cloned.1.call-start = ((), (), s32[]{:S(2)}) async-start(), calls=%async_computation.17 | async-start | bytes 2359296 | tf_op jit(solution)/shard_map/reduce_scatter | solution.py:262
  957.9 256.0 %reduce-scatter.10.cloned.1.call-start = ((), (), s32[]{:S(2)}) async-start(), calls=%async_computation.18 | async-start | bytes 2359296 | tf_op jit(solution)/shard_map/reduce_scatter | solution.py:265
  960.3 324.3 %reduce-scatter.12.cloned.1.call-start = ((), (), s32[]{:S(2)}) async-start(), calls=%async_computation.19 | async-start | bytes 2359296 | tf_op jit(solution)/shard_map/reduce_scatter | solution.py:268
  962.7 473.8 %reduce-scatter.16.cloned.1.call-start = ((), (), s32[]{:S(2)}) async-start(), calls=%async_computation.21 | async-start | bytes 9437184 | tf_op jit(solution)/shard_map/reduce_scatter | solution.py:274
  969.6 618.4 %reduce-scatter.18.cloned.1.call-start = ((), (), s32[]{:S(2)}) async-start(), calls=%async_computation.22 | async-start | bytes 9437184 | tf_op jit(solution)/shard_map/reduce_scatter | solution.py:277
  976.5 763.9 %reduce-scatter.20.cloned.1.call-start = ((), (), s32[]{:S(2)}) async-start(), calls=%async_computation.23 | async-start | bytes 9437184 | tf_op jit(solution)/shard_map/reduce_scatter | solution.py:280
  (36 other events, 335.3 us)
Sparse Core Ops, SparseCore 0:
  10.1 52.0 all-gather.10
  64.3 47.7 all-gather.16
  114.3 47.7 all-gather.12
  165.4 44.4 all-gather.14
  211.7 49.7 all-gather.18
  265.3 49.5 all-reduce.11
  317.3 125.0 all-gather.20
  444.7 123.1 all-gather.22
  570.0 123.5 all-gather.24
  713.0 49.5 all-reduce.13
  950.0 49.4 all-reduce.15
  1003.4 68.4 reduce-scatter.13
  1076.4 66.8 reduce-scatter.7
  1147.1 66.8 reduce-scatter.9
  1217.7 66.8 reduce-scatter.11
  1288.5 147.9 reduce-scatter.15
  1440.0 147.9 reduce-scatter.17
  1592.0 148.4 reduce-scatter.19
where the time goes:
time: 1760 us; the launch traced here: 1750 us
  waiting for transfers between devices  1470 us (84%)
  matrix products  106 us (6%)
  other arithmetic  63.6 us (4%)
  blocking collectives  62.5 us (4%)
  local copies, waits for them, and re-layouts  28.8 us (2%)
    reduce_scatter x1, waiting for transfers between devices, per_device(): lax.psum_scatter(gate_wgrad.astype(jnp.bfloat16), ('seq', 'ctx'), scatter...  150 us
    reduce_scatter x1, waiting for transfers between devices, per_device(): lax.psum_scatter(down_grad.astype(jnp.bfloat16), ('seq', 'ctx'), scatter_...  150 us
    reduce_scatter x1, waiting for transfers between devices, per_device(): lax.psum_scatter(upward_wgrad.astype(jnp.bfloat16), ('seq', 'ctx'), scatt...  149 us
    ppermute x8, waiting for transfers between devices, shifted(): return lax.ppermute(block, axis, route)  135 us
    all_gather x1, waiting for transfers between devices, per_device(): lax.all_gather(gate_weight, ('seq', 'ctx'), axis=0, tiled=True)  125 us
    all_gather x1, waiting for transfers between devices, per_device(): lax.all_gather(down_weight, ('seq', 'ctx'), axis=1, tiled=True)  119 us
    all_gather x1, waiting for transfers between devices, per_device(): lax.all_gather(up_weight, ('seq', 'ctx'), axis=0, tiled=True)  118 us
    reduce_scatter x1, waiting for transfers between devices, per_device(): lax.psum_scatter(query_wgrad.astype(jnp.bfloat16), ('seq', 'ctx'), scatte...  69.6 us
  transfers between devices with their start and end apart: 26, of which 22 were waited for; matrix products, arithmetic and copies ran while one was open for 7% of the time, Pallas kernels for 0%

commit v1 on v0

--- a/solution.py
+++ b/solution.py
@@ -8,6 +8,16 @@
 BLOCK = 128
 THETA = 130000.0
 EPS = 1e-05
+
+
+def collect(x, axis, dim):
+    ways, here, step = (lax.axis_size(axis), lax.axis_index(axis), x.shape[dim])
+    shape = [n * ways if d == dim else n for d, n in enumerate(x.shape)]
+    full = lax.dynamic_update_slice_in_dim(jnp.zeros(shape, x.dtype), x, here * step, axis=dim)
+    for far in range(1, ways):
+        x = lax.ppermute(x, axis, [(d, (d + 1) % ways) for d in range(ways)])
+        full = lax.dynamic_update_slice_in_dim(full, x, (here - far) % ways * step, axis=dim)
+    return full
 
 
 def shifted(block, axis, distance):
@@ -94,7 +104,7 @@
     gathered = (
         lax.all_gather(query_weight, ("seq", "ctx"), axis=0, tiled=True),
         lax.all_gather(key_weight, ("seq", "ctx"), axis=0, tiled=True),
-        lax.all_gather(value_weight, ("seq", "ctx"), axis=0, tiled=True),
+        collect(value_weight, ("seq", "ctx"), 0),
         lax.all_gather(output_weight, ("seq", "ctx"), axis=1, tiled=True),
         lax.all_gather(gate_weight, ("seq", "ctx"), axis=0, tiled=True),
         lax.all_gather(up_weight, ("seq", "ctx"), axis=0, tiled=True),

time: 1760 us -> 1760 us (level)
    ppermute x0 -> x7, waiting for transfers between devices: none -> 70.3 us  [collect(): x = lax.ppermute(x, axis, [(d, (d + 1) % ways) for d in range(ways)])]
    all_gather x1, waiting for transfers between devices: 47.4 us -> 7.93 us  [per_device(): lax.all_gather(query_weight, ('seq', 'ctx'), axis=0, tiled=True)]
    all_gather x1, waiting for transfers between devices: 39 us -> 0.01 us  [per_device(): lax.all_gather(value_weight, ('seq', 'ctx'), axis=0, tiled=True)]
    all_gather x1, waiting for transfers between devices: 27.6 us -> 0.02 us  [per_device(): lax.all_gather(key_weight, ('seq', 'ctx'), axis=0, tiled=True)]
    ppermute x8, waiting for transfers between devices: 135 us -> 162 us  [shifted(): return lax.ppermute(block, axis, route)]
  transfers between devices with their start and end apart: 26 -> 33, of which waited for: 22 -> 26; matrix products, arithmetic and copies ran while one was open for 7% -> 9% of each run, Pallas kernels for 0% -> 0%
where the time goes in v1:
time: 1760 us; the launch traced here: 1750 us
  waiting for transfers between devices  1460 us (83%)
  matrix products  108 us (6%)
  blocking collectives  63.8 us (4%)
  other arithmetic  61.1 us (3%)
  local copies, waits for them, and re-layouts  30.3 us (2%)
    ppermute x8, waiting for transfers between devices, shifted(): return lax.ppermute(block, axis, route)  162 us
    reduce_scatter x1, waiting for transfers between devices, per_device(): lax.psum_scatter(upward_wgrad.astype(jnp.bfloat16), ('seq', 'ctx'), scatt...  150 us
    reduce_scatter x1, waiting for transfers between devices, per_device(): lax.psum_scatter(down_grad.astype(jnp.bfloat16), ('seq', 'ctx'), scatter_...  150 us
    reduce_scatter x1, waiting for transfers between devices, per_device(): lax.psum_scatter(gate_wgrad.astype(jnp.bfloat16), ('seq', 'ctx'), scatter...  149 us
    all_gather x1, waiting for transfers between devices, per_device(): lax.all_gather(gate_weight, ('seq', 'ctx'), axis=0, tiled=True)  124 us
    all_gather x1, waiting for transfers between devices, per_device(): lax.all_gather(down_weight, ('seq', 'ctx'), axis=1, tiled=True)  119 us
    all_gather x1, waiting for transfers between devices, per_device(): lax.all_gather(up_weight, ('seq', 'ctx'), axis=0, tiled=True)  118 us
    ppermute x7, waiting for transfers between devices, collect(): x = lax.ppermute(x, axis, [(d, (d + 1) % ways) for d in range(ways)])  70.3 us
  transfers between devices with their start and end apart: 33, of which 26 were waited for; matrix products, arithmetic and copies ran while one was open for 9% of the time, Pallas kernels for 0%

profile of v1, /device:TPU:0, one launch (start us, length us, event | category | flops | bytes accessed | tf_op | source)
XLA Modules:
  0.0 1748.1 jit_solution(11240490849333565688)
XLA Ops:
  12.0 9.4 collective-permute-done.2
  22.3 15.9 collective-permute-done.3
  39.5 7.9 collective-permute-done.4
  47.5 16.1 collective-permute-done.5
  63.8 23.6 %all-gather = bf16[8,1,256]{2,1,0:T(2,128)(2,1)S(1)} all-gather(bf16[1,1,256]{2,1,0:T(2,128)(2,1)S(1)} %reshape.359), channel_id=1, replica_groups=mesh['seq'=2,'ctx'=4,'tp'=4] {'seq','ctx'}, dimensions={0}, use_global_device_ids=true | all-gather | bytes 4608 | tf_op jit(solution)/shard_map/all_gather | solution.py:112
  94.5 9.5 collective-permute-done.7
  106.0 11.6 collective-permute-done.8
  121.0 7.9 all-gather.15.cloned.1.call-done
  134.6 45.1 %all-gather.13.cloned.1.call-done = bf16[2,1024,512]{2,1,0:T(8,128)(2,1)} async-done(((bf16[2,256,512]{2,1,0:T(8,128)(2,1)}), bf16[2,1024,512]{2,1,0:T(8,128)(2,1)}) %all-gather.13.cloned.1.call-update) | async-done | bytes 2097168 | tf_op jit(solution)/shard_map/all_gather | solution.py:142
  179.7 22.9 %while.39 = (s32[]{:T(128)}, f32[256,8]{0,1:T(8,128)S(1)}, f32[256,512]{0,1:T(8,128)}, s32[256]{0:T(256)}, s32[8]{0:T(128)}, /*index=5*/bf16[2,1024,512]{2,1,0:T...) while((s32[]{:T(128)}, f32[256,8]{0,1:T(8,128)S(1)}, ...), condition=%wide.region_5.6_spmd.clone, body=%wide.region_2.5_spmd.clone.sunk | while | flops 137706752 | bytes 9411818 | solution.py:161
  203.6 27.7 %all-gather.17.cloned.1.call-done = bf16[512,2048]{1,0:T(8,128)(2,1)} async-done(((bf16[512,256]{1,0:T(8,128)(2,1)}), bf16[512,2048]{1,0:T(8,128)(2,1)}) %all-gather.17.cloned.1.call-update) | async-done | bytes 2097168 | tf_op jit(solution)/shard_map/all_gather | solution.py:108
  237.2 18.2 %all-gather.1 = bf16[8,1,256]{2,1,0:T(2,128)(2,1)S(1)} all-gather(bf16[1,1,256]{2,1,0:T(2,128)(2,1)S(1)} %reshape.361), channel_id=1, replica_groups=mesh['seq'=2,'ctx'=4,'tp'=4] {'seq','ctx'}, dimensions={0}, use_global_device_ids=true | all-gather | bytes 4608 | tf_op jit(solution)/shard_map/all_gather | solution.py:113
  256.0 28.8 %all-reduce.12.cloned.1.call-done = f32[256,2048]{1,0:T(8,128)} async-done(((f32[256,2048]{1,0:T(8,128)}), f32[256,2048]{1,0:T(8,128)}) %all-reduce.12.cloned.1.call-update) | async-done | bytes 2097168 | tf_op jit(solution)/shard_map/psum | solution.py:166
  287.6 124.4 %all-gather.19.cloned.1.call-done = bf16[2048,2048]{1,0:T(8,128)(2,1)} async-done(((bf16[256,2048]{1,0:T(8,128)(2,1)}), bf16[2048,2048]{1,0:T(8,128)(2,1)}) %all-gather.19.cloned.1.call-update) | async-done | bytes 8388624 | tf_op jit(solution)/shard_map/all_gather | solution.py:109
  419.0 118.5 %all-gather.21.cloned.1.call-done = bf16[2048,2048]{1,0:T(8,128)(2,1)} async-done(((bf16[256,2048]{1,0:T(8,128)(2,1)}), bf16[2048,2048]{1,0:T(8,128)(2,1)}) %all-gather.21.cloned.1.call-update) | async-done | bytes 8388624 | tf_op jit(solution)/shard_map/all_gather | solution.py:110
  544.5 118.8 %all-gather.23.cloned.1.call-done = bf16[2048,2048]{1,0:T(8,128)(2,1)} async-done(((bf16[2048,256]{1,0:T(8,128)(2,1)}), bf16[2048,2048]{1,0:T(8,128)(2,1)}) %all-gather.23.cloned.1.call-update) | async-done | bytes 8388624 | tf_op jit(solution)/shard_map/all_gather | solution.py:111
  663.3 9.0 multiply_convert_fusion.1
  692.1 40.3 %all-reduce.14.cloned.1.call-done = f32[256,2048]{1,0:T(8,128)} async-done(((f32[256,2048]{1,0:T(8,128)}), f32[256,2048]{1,0:T(8,128)}) %all-reduce.14.cloned.1.call-update) | async-done | bytes 2097168 | tf_op jit(solution)/shard_map/psum | solution.py:205
  738.5 199.0 %while.40 = (s32[]{:T(128)}, bf16[2,256,512]{1,2,0:T(8,128)(2,1)}, f32[2,256,512]{1,2,0:T(8,128)S(1)}, f32[256,8,64]{0,2,1:T(8,128)}, s32[256]{0:T(256)}, /*inde...) while((s32[]{:T(128)}, bf16[2,256,512]{1,2,0:T(8,128)(2,1)}, ...), condition=%wide.region_14.15_spmd.clone, body=%wide.region_12.14_spmd.clone.sunk | while | flops 340866304 | bytes 25116048 | solution.py:254
  749.2 56.9 %collective-permute-done = bf16[2,256,512]{1,2,0:T(8,128)(2,1)} collective-permute-done((bf16[2,256,512]{1,2,0:T(8,128)(2,1)S(1)}, bf16[2,256,512]{1,2,0:T(8,128)(2,1)}, u32[]{:S(2)}, u32[]{:S(2)}) %collective-permute-start) | collective-permute-done | bytes 524320 | tf_op jit(solution)/shard_map/while/body/eval_jaxpr/ppermute | solution.py:26
  815.4 35.4 %collective-permute-done = bf16[2,256,512]{1,2,0:T(8,128)(2,1)} collective-permute-done((bf16[2,256,512]{1,2,0:T(8,128)(2,1)S(1)}, bf16[2,256,512]{1,2,0:T(8,128)(2,1)}, u32[]{:S(2)}, u32[]{:S(2)}) %collective-permute-start) | collective-permute-done | bytes 524320 | tf_op jit(solution)/shard_map/while/body/eval_jaxpr/ppermute | solution.py:26
  859.6 35.0 %collective-permute-done = bf16[2,256,512]{1,2,0:T(8,128)(2,1)} collective-permute-done((bf16[2,256,512]{1,2,0:T(8,128)(2,1)S(1)}, bf16[2,256,512]{1,2,0:T(8,128)(2,1)}, u32[]{:S(2)}, u32[]{:S(2)}) %collective-permute-start) | collective-permute-done | bytes 524320 | tf_op jit(solution)/shard_map/while/body/eval_jaxpr/ppermute | solution.py:26
  903.4 34.1 %collective-permute-done = bf16[2,256,512]{1,2,0:T(8,128)(2,1)} collective-permute-done((bf16[2,256,512]{1,2,0:T(8,128)(2,1)S(1)}, bf16[2,256,512]{1,2,0:T(8,128)(2,1)}, u32[]{:S(2)}, u32[]{:S(2)}) %collective-permute-start) | collective-permute-done | bytes 524320 | tf_op jit(solution)/shard_map/while/body/eval_jaxpr/ppermute | solution.py:26
  983.9 13.8 all-reduce.16.cloned.1.call-done
  1000.0 22.1 %all-reduce.6 = (bf16[2048]{0:T(1024)(128)(2,1)S(1)}, bf16[2048]{0:T(1024)(128)(2,1)S(1)}) all-reduce(bf16[2048]{0:T(1024)(128)(2,1)S(1)} %get-tuple-element.603, bf16[2048]{0:T(1024)(128)(2,1)S(1)} %copy-done.35), channel_id=9, replica_groups=mesh['seq'=2,'ctx'=4,'tp'=4] {'seq','ctx'}, use_global_device_ids=true, to_apply=%region_25.26.clone | all-reduce | flops 4096 | bytes 16384
  1028.0 42.1 %reduce-scatter.14.cloned.1.call-done = bf16[512,256]{1,0:T(8,128)(2,1)} async-done(((bf16[512,2048]{1,0:T(8,128)(2,1)}), bf16[512,256]{1,0:T(8,128)(2,1)}) %reduce-scatter.14.cloned.1.call-update) | async-done | bytes 262160 | tf_op jit(solution)/shard_map/reduce_scatter | solution.py:281
  1071.8 69.6 %reduce-scatter.8.cloned.1.call-done = bf16[256,512]{1,0:T(8,128)(2,1)} async-done(((bf16[2048,512]{1,0:T(8,128)(2,1)}), bf16[256,512]{1,0:T(8,128)(2,1)}) %reduce-scatter.8.cloned.1.call-update) | async-done | bytes 262160 | tf_op jit(solution)/shard_map/reduce_scatter | solution.py:272
  1143.2 68.8 %reduce-scatter.10.cloned.1.call-done = bf16[256,512]{1,0:T(8,128)(2,1)} async-done(((bf16[2048,512]{1,0:T(8,128)(2,1)}), bf16[256,512]{1,0:T(8,128)(2,1)}) %reduce-scatter.10.cloned.1.call-update) | async-done | bytes 262160 | tf_op jit(solution)/shard_map/reduce_scatter | solution.py:275
  1213.8 68.7 %reduce-scatter.12.cloned.1.call-done = bf16[256,512]{1,0:T(8,128)(2,1)} async-done(((bf16[2048,512]{1,0:T(8,128)(2,1)}), bf16[256,512]{1,0:T(8,128)(2,1)}) %reduce-scatter.12.cloned.1.call-update) | async-done | bytes 262160 | tf_op jit(solution)/shard_map/reduce_scatter | solution.py:278
  1284.3 150.1 %reduce-scatter.18.cloned.1.call-done = bf16[256,2048]{1,0:T(8,128)(2,1)} async-done(((bf16[2048,2048]{1,0:T(8,128)(2,1)}), bf16[256,2048]{1,0:T(8,128)(2,1)}) %reduce-scatter.18.cloned.1.call-update) | async-done | bytes 1048592 | tf_op jit(solution)/shard_map/reduce_scatter | solution.py:287
  1437.2 148.8 %reduce-scatter.16.cloned.1.call-done = bf16[256,2048]{1,0:T(8,128)(2,1)} async-done(((bf16[2048,2048]{1,0:T(8,128)(2,1)}), bf16[256,2048]{1,0:T(8,128)(2,1)}) %reduce-scatter.16.cloned.1.call-update) | async-done | bytes 1048592 | tf_op jit(solution)/shard_map/reduce_scatter | solution.py:284
  1588.8 149.6 %reduce-scatter.20.cloned.1.call-done = bf16[2048,256]{1,0:T(8,128)(2,1)} async-done(((bf16[2048,2048]{1,0:T(8,128)(2,1)}), bf16[2048,256]{1,0:T(8,128)(2,1)}) %reduce-scatter.20.cloned.1.call-update) | async-done | bytes 1048592 | tf_op jit(solution)/shard_map/reduce_scatter | solution.py:290
  (321 shorter events, 204.4 us)
Async XLA Ops:
  7.2 111.2 %all-gather.11.cloned.1.call-start = ((), (), s32[]{:S(2)}) async-start(), calls=%async_computation.7 | async-start | bytes 2359296 | tf_op jit(solution)/shard_map/all_gather | solution.py:106
  7.9 121.0 %all-gather.15.cloned.1.call-start = ((), (), s32[]{:S(2)}) async-start(), calls=%async_computation.9 | async-start | bytes 2359296 | tf_op jit(solution)/shard_map/all_gather | solution.py:105
  8.7 171.0 %all-gather.13.cloned.1.call-start = ((), (), s32[]{:S(2)}) async-start(), calls=%async_computation.8 | async-start | bytes 2621440 | tf_op jit(solution)/shard_map/all_gather | solution.py:142
  8.7 12.7 collective-permute-start.2
  21.4 16.8 collective-permute-start.3
  47.4 16.2 collective-permute-start.5
  63.5 27.4 %collective-permute-start.6 = (bf16[256,512]{1,0:T(8,128)(2,1)}, bf16[256,512]{1,0:T(8,128)(2,1)}, u32[]{:S(2)}, u32[]{:S(2)}) collective-permute-start(bf16[256,512]{1,0:T(8,128)(2,1)} %collective-permute-done.5), channel_id=1, source_target_pairs={{0,4},{4,8},{8,12},{12,16},{16,20},{20,24},{24,28},{28,0},{1,5},{5... | collective-permute-start | bytes 786440 | tf_op jit(solution)/shard_map/ppermute | solution.py:18
  91.0 13.0 collective-permute-start.7
  104.0 13.6 collective-permute-start.8
  133.8 97.6 %all-gather.17.cloned.1.call-start = ((), (), s32[]{:S(2)}) async-start(), calls=%async_computation.10 | async-start | bytes 2359296 | tf_op jit(solution)/shard_map/all_gather | solution.py:108
  134.4 150.4 %all-reduce.12.cloned.1.call-start = ((), (), s32[]{:S(2)}) async-start(), calls=%async_computation.11 | async-start | bytes 4194304 | tf_op jit(solution)/shard_map/psum | solution.py:166
  235.1 177.0 %all-gather.19.cloned.1.call-start = ((), (), s32[]{:S(2)}) async-start(), calls=%async_computation.12 | async-start | bytes 9437184 | tf_op jit(solution)/shard_map/all_gather | solution.py:109
  235.6 301.9 %all-gather.21.cloned.1.call-start = ((), (), s32[]{:S(2)}) async-start(), calls=%async_computation.13 | async-start | bytes 9437184 | tf_op jit(solution)/shard_map/all_gather | solution.py:110
  236.4 426.9 %all-gather.23.cloned.1.call-start = ((), (), s32[]{:S(2)}) async-start(), calls=%async_computation.14 | async-start | bytes 9437184 | tf_op jit(solution)/shard_map/all_gather | solution.py:111
  237.1 495.2 %all-reduce.14.cloned.1.call-start = ((), (), s32[]{:S(2)}) async-start(), calls=%async_computation.15 | async-start | bytes 4194304 | tf_op jit(solution)/shard_map/psum | solution.py:205
  682.6 261.5 %all-gather.25.cloned.1.call-start = ((), (), s32[]{:S(2)}) async-start(), calls=%async_computation.16 | async-start | bytes 2359296 | tf_op jit(solution)/shard_map/all_gather | solution.py:179
  683.2 314.5 %all-reduce.16.cloned.1.call-start = ((), (), s32[]{:S(2)}) async-start(), calls=%async_computation.24 | async-start | bytes 4194304 | tf_op jit(solution)/shard_map/psum | solution.py:173
  745.0 61.1 %collective-permute-start.1 = (f32[2,256,512]{1,2,0:T(8,128)}, f32[2,256,512]{1,2,0:T(8,128)S(1)}, u32[]{:S(2)}, u32[]{:S(2)}) collective-permute-start(f32[2,256,512]{1,2,0:T(8,128)} %maximum_add_fusion.2), channel_id=1, source_target_pairs={{12,0},{0,4},{4,8},{8,12},{13,1},{1,5},{5,9},{9,13},{14,2},{2,6},{... | collective-permute-start | bytes 3145736 | tf_op jit(solution)/shard_map/while/body/eval_jaxpr/ppermute | solution.py:26
  746.5 59.7 %collective-permute-start = (bf16[2,256,512]{1,2,0:T(8,128)(2,1)S(1)}, bf16[2,256,512]{1,2,0:T(8,128)(2,1)}, u32[]{:S(2)}, u32[]{:S(2)}) collective-permute-start(bf16[2,256,512]{1,2,0:T(8,128)(2,1)S(1)} %copy.103), channel_id=1, source_target_pairs={{12,0},{0,4},{4,8},{8,12},{13,1},{1,5},{5,9},{9,13},{14,2},{2,6},{... | collective-permute-start | bytes 1572872 | tf_op jit(solution)/shard_map/while/body/eval_jaxpr/ppermute | solution.py:26
  812.6 38.2 %collective-permute-start.1 = (f32[2,256,512]{1,2,0:T(8,128)}, f32[2,256,512]{1,2,0:T(8,128)S(1)}, u32[]{:S(2)}, u32[]{:S(2)}) collective-permute-start(f32[2,256,512]{1,2,0:T(8,128)} %maximum_add_fusion.2), channel_id=1, source_target_pairs={{12,0},{0,4},{4,8},{8,12},{13,1},{1,5},{5,9},{9,13},{14,2},{2,6},{... | collective-permute-start | bytes 3145736 | tf_op jit(solution)/shard_map/while/body/eval_jaxpr/ppermute | solution.py:26
  812.6 38.2 %collective-permute-start = (bf16[2,256,512]{1,2,0:T(8,128)(2,1)S(1)}, bf16[2,256,512]{1,2,0:T(8,128)(2,1)}, u32[]{:S(2)}, u32[]{:S(2)}) collective-permute-start(bf16[2,256,512]{1,2,0:T(8,128)(2,1)S(1)} %copy.103), channel_id=1, source_target_pairs={{12,0},{0,4},{4,8},{8,12},{13,1},{1,5},{5,9},{9,13},{14,2},{2,6},{... | collective-permute-start | bytes 1572872 | tf_op jit(solution)/shard_map/while/body/eval_jaxpr/ppermute | solution.py:26
  857.3 37.3 %collective-permute-start.1 = (f32[2,256,512]{1,2,0:T(8,128)}, f32[2,256,512]{1,2,0:T(8,128)S(1)}, u32[]{:S(2)}, u32[]{:S(2)}) collective-permute-start(f32[2,256,512]{1,2,0:T(8,128)} %maximum_add_fusion.2), channel_id=1, source_target_pairs={{12,0},{0,4},{4,8},{8,12},{13,1},{1,5},{5,9},{9,13},{14,2},{2,6},{... | collective-permute-start | bytes 3145736 | tf_op jit(solution)/shard_map/while/body/eval_jaxpr/ppermute | solution.py:26
  857.3 37.3 %collective-permute-start = (bf16[2,256,512]{1,2,0:T(8,128)(2,1)S(1)}, bf16[2,256,512]{1,2,0:T(8,128)(2,1)}, u32[]{:S(2)}, u32[]{:S(2)}) collective-permute-start(bf16[2,256,512]{1,2,0:T(8,128)(2,1)S(1)} %copy.103), channel_id=1, source_target_pairs={{12,0},{0,4},{4,8},{8,12},{13,1},{1,5},{5,9},{9,13},{14,2},{2,6},{... | collective-permute-start | bytes 1572872 | tf_op jit(solution)/shard_map/while/body/eval_jaxpr/ppermute | solution.py:26
  901.1 36.4 %collective-permute-start.1 = (f32[2,256,512]{1,2,0:T(8,128)}, f32[2,256,512]{1,2,0:T(8,128)S(1)}, u32[]{:S(2)}, u32[]{:S(2)}) collective-permute-start(f32[2,256,512]{1,2,0:T(8,128)} %maximum_add_fusion.2), channel_id=1, source_target_pairs={{12,0},{0,4},{4,8},{8,12},{13,1},{1,5},{5,9},{9,13},{14,2},{2,6},{... | collective-permute-start | bytes 3145736 | tf_op jit(solution)/shard_map/while/body/eval_jaxpr/ppermute | solution.py:26
  901.1 36.4 %collective-permute-start = (bf16[2,256,512]{1,2,0:T(8,128)(2,1)S(1)}, bf16[2,256,512]{1,2,0:T(8,128)(2,1)}, u32[]{:S(2)}, u32[]{:S(2)}) collective-permute-start(bf16[2,256,512]{1,2,0:T(8,128)(2,1)S(1)} %copy.103), channel_id=1, source_target_pairs={{12,0},{0,4},{4,8},{8,12},{13,1},{1,5},{5,9},{9,13},{14,2},{2,6},{... | collective-permute-start | bytes 1572872 | tf_op jit(solution)/shard_map/while/body/eval_jaxpr/ppermute | solution.py:26
  948.1 122.0 %reduce-scatter.14.cloned.1.call-start = ((), (), s32[]{:S(2)}) async-start(), calls=%async_computation.20 | async-start | bytes 2359296 | tf_op jit(solution)/shard_map/reduce_scatter | solution.py:281
  952.7 188.8 %reduce-scatter.8.cloned.1.call-start = ((), (), s32[]{:S(2)}) async-start(), calls=%async_computation.17 | async-start | bytes 2359296 | tf_op jit(solution)/shard_map/reduce_scatter | solution.py:272
  956.1 255.9 %reduce-scatter.10.cloned.1.call-start = ((), (), s32[]{:S(2)}) async-start(), calls=%async_computation.18 | async-start | bytes 2359296 | tf_op jit(solution)/shard_map/reduce_scatter | solution.py:275
  958.4 324.0 %reduce-scatter.12.cloned.1.call-start = ((), (), s32[]{:S(2)}) async-start(), calls=%async_computation.19 | async-start | bytes 2359296 | tf_op jit(solution)/shard_map/reduce_scatter | solution.py:278
  960.9 473.5 %reduce-scatter.18.cloned.1.call-start = ((), (), s32[]{:S(2)}) async-start(), calls=%async_computation.22 | async-start | bytes 9437184 | tf_op jit(solution)/shard_map/reduce_scatter | solution.py:287
  967.8 618.1 %reduce-scatter.16.cloned.1.call-start = ((), (), s32[]{:S(2)}) async-start(), calls=%async_computation.21 | async-start | bytes 9437184 | tf_op jit(solution)/shard_map/reduce_scatter | solution.py:284
  974.8 763.5 %reduce-scatter.20.cloned.1.call-start = ((), (), s32[]{:S(2)}) async-start(), calls=%async_computation.23 | async-start | bytes 9437184 | tf_op jit(solution)/shard_map/reduce_scatter | solution.py:290
  (44 other events, 1215.4 us)
Sparse Core Ops, SparseCore 0:
  10.2 63.7 all-gather.10
  76.1 52.8 all-gather.14
  133.9 45.7 all-gather.12
  181.5 49.7 all-gather.16
  235.1 49.5 all-reduce.11
  286.9 125.0 all-gather.18
  414.3 123.1 all-gather.20
  539.7 123.5 all-gather.22
  682.7 49.5 all-reduce.13
  734.3 70.0 all-gather.24
  948.2 49.4 all-reduce.15
  1001.5 68.4 reduce-scatter.13
  1074.6 66.8 reduce-scatter.7
  1145.2 66.7 reduce-scatter.9
  1215.8 66.6 reduce-scatter.11
  1286.4 147.9 reduce-scatter.17
  1437.9 148.0 reduce-scatter.15
  1589.9 148.3 reduce-scatter.19
